TPU v7x, 32 devices: a whole 2x2x4 slice. The times are simulated.
32 devices in a mesh: img: 8 (over z, core), pix: 4 (over y, x).
Axes of the slice: x: 2, y: 2, z: 4, core: 2. Of those that a mesh axis runs over, the one named last changes fastest.
Arguments:
- images: bfloat16 [25600, 16384], P('img', 'pix'), may hold values from -6 to 6
- classes: int32 [25600], P('img'), may hold values from 0 to 63
- ctf_table: bfloat16 [64, 16384], P(None, 'pix'), may hold values from -1 to 1, as said below
- weights: float32 [25600], P('img'), may hold values from 0.1 to 1
- probes: float32 [16384, 256], P('pix'), may hold values from -6 to 6
Outputs:
- basis: float32 [16384, 256], P('pix')
- factor: float32 [256, 256], replicated
Inputs may be any that keep to these rules, and one draw needn't show every extreme that they name: `ctf_table`: a smooth envelope over the pixel index times an independent magnitude and sign for each entry.
All inputs are finite; a program needn't handle non-finite values.
Results may differ from a plain program's by a relative error of at most 0.012.
Values may be sent and summed in bfloat16 or wider, within the bound.
No kernel may reach another device: no remote copies, remote signals or barrier semaphores. Data moves between devices by JAX's collectives and lax.ppermute only.
A program may use at most 128 MiB of HBM per device.

v0:
```python
import jax
import jax.numpy as jnp
from jax import lax
from jax.sharding import PartitionSpec as P

ITERS = 2


def per_device(images, classes, ctf_table, weights, probes):
    onehot = (classes[:, None] == jnp.arange(ctf_table.shape[0])[None, :]).astype(jnp.bfloat16)
    filters = jnp.dot(onehot, ctf_table, preferred_element_type=jnp.float32)
    filtered = (images.astype(jnp.float32) * filters).astype(jnp.bfloat16)
    current = probes
    factor = jnp.zeros((probes.shape[1], probes.shape[1]), jnp.float32)
    for sweep in range(ITERS):
        probe_half = current.astype(jnp.bfloat16)
        share_rows = filtered.shape[0] // lax.axis_size("pix")
        shares = lax.psum_scatter(
            jnp.dot(filtered, probe_half, preferred_element_type=jnp.float32),
            "pix",
            scatter_dimension=0,
            tiled=True,
        )
        weight_share = lax.dynamic_slice_in_dim(
            weights, lax.axis_index("pix") * share_rows, share_rows, 0
        )
        scaled_share = (weight_share[:, None] * shares).astype(jnp.bfloat16)
        scaled = lax.all_gather(scaled_share, "pix", axis=0, tiled=True)
        partial_sum = lax.dot_general(
            filtered, scaled, (((0,), (0,)), ((), ())), preferred_element_type=jnp.float32
        )
        image_sum = lax.psum(partial_sum, "img")
        gram_matrix = lax.psum(
            jnp.dot(image_sum.T, image_sum, precision=lax.Precision.HIGHEST), "pix"
        )
        factor = jnp.linalg.cholesky(gram_matrix)
        current = jax.scipy.linalg.solve_triangular(factor, image_sum.T, lower=True).T
    return (current, factor)


def solution(mesh):
    in_specs = (P("img", "pix"), P("img"), P(None, "pix"), P("img"), P("pix", None))
    out_specs = (P("pix", None), P())
    return jax.shard_map(
        per_device, mesh=mesh, in_specs=in_specs, out_specs=out_specs, check_vma=False
    )
```

profile of v0, /device:TPU:0, one launch (start us, length us, event | category | flops | bytes accessed | tf_op | source)
XLA Modules:
  0.0 707.9 jit_solution(17062650772016324928)
XLA Ops:
  7.2 1.0 copy-done
  8.2 21.5 %multiply_convert_fusion = bf16[3200,4096]{1,0:T(8,128)(2,1)} fusion(bf16[3200,4096]{1,0:T(8,128)(2,1)} %param.8, bf16[64,4096]{1,0:T(8,128)(2,1)S(1)} %copy-done, s32[3200]{0:T(1024)} %param.9), kind=kOutput, calls=%fused_computation.4 | convolution fusion | flops 1717248000 | bytes 52965888 | tf_op jit(solution)/shard_map/dot_general | solution.py:11
  29.7 14.4 %fusion.5 = f32[3200,256]{1,0:T(8,128)} fusion(bf16[3200,4096]{1,0:T(8,128)(2,1)} %multiply_convert_fusion, f32[4096,256]{1,0:T(8,128)} %param.12), kind=kOutput, calls=%fused_computation.14 | convolution fusion | flops 6711934976 | bytes 33685504 | tf_op jit(solution)/shard_map/dot_general | solution.py:19
  44.2 0.8 dynamic_slice.4
  45.0 47.0 %reduce-scatter.3.cloned.1.call-done = f32[800,256]{1,0:T(8,128)} async-done(((f32[3200,256]{1,0:T(8,128)}), f32[800,256]{1,0:T(8,128)}) %reduce-scatter.3.cloned.1.call-update) | async-done | bytes 819216 | tf_op jit(solution)/shard_map/reduce_scatter | solution.py:18
  92.0 2.1 multiply_convert_fusion.2
  94.1 0.0 all-reduce.6.cloned.1.call-start
  94.2 31.7 %all-gather.3.cloned.1.call-done = bf16[3200,256]{1,0:T(8,128)(2,1)} async-done(((bf16[800,256]{1,0:T(8,128)(2,1)}), bf16[3200,256]{1,0:T(8,128)(2,1)}) %all-gather.3.cloned.1.call-update) | async-done | bytes 1638416 | tf_op jit(solution)/shard_map/all_gather | solution.py:28
  125.9 14.4 %fusion.30 = f32[4096,256]{1,0:T(8,128)} fusion(bf16[3200,4096]{1,0:T(8,128)(2,1)} %multiply_convert_fusion, bf16[3200,256]{1,0:T(8,128)(2,1)} %all-gather.3.cloned.1.call-done), kind=kOutput, calls=%fused_computation.66 | convolution fusion | flops 6710886400 | bytes 32047104 | tf_op jit(solution)/shard_map/dot_general | solution.py:29
  140.3 0.5 all-reduce.8.cloned.1.call-start
  140.8 96.1 %all-reduce.6.cloned.1.call-done = f32[4096,256]{1,0:T(8,128)} async-done(((f32[4096,256]{1,0:T(8,128)}), f32[4096,256]{1,0:T(8,128)}) %all-reduce.6.cloned.1.call-update) | async-done | bytes 4194320 | tf_op jit(solution)/shard_map/psum | solution.py:32
  236.9 10.9 %fusion.31 = f32[256,256]{0,1:T(8,128)} fusion(f32[4096,256]{1,0:T(8,128)} %all-reduce.6.cloned.1.call-done), kind=kOutput, calls=%fused_computation.67 | convolution fusion | flops 3221225472 | bytes 4456448 | tf_op jit(solution)/shard_map/dot_general | solution.py:34
  247.9 0.2 reduce-scatter.5.cloned.1.call-start
  248.1 43.0 %all-reduce.8.cloned.1.call-done = f32[256,256]{0,1:T(8,128)} async-done(((f32[256,256]{0,1:T(8,128)}), f32[256,256]{0,1:T(8,128)}) %all-reduce.8.cloned.1.call-update) | async-done | bytes 262160 | tf_op jit(solution)/shard_map/psum | solution.py:33
  291.1 1.1 copy.8
  292.2 1.0 fusion.9
  293.2 11.7 %cholesky.130 = f32[128,128]{1,0:T(8,128)S(1)} custom-call(f32[128,128]{1,0:T(8,128)S(1)} %cholesky.194), custom_call_target="Cholesky" | custom-call | tf_op jit(solution)/shard_map/jit(cholesky)/cholesky | solution.py:36
  305.0 9.8 %custom-call.13 = f32[1,128,128]{1,2,0:T(8,128)S(1)} custom-call(f32[1,128,128]{2,1,0:T(8,128)S(1)} %get-tuple-element.51), custom_call_target="InvertDiagBlocksLowerTriangular" | custom-call | tf_op jit(solution)/shard_map/jit(cholesky)/cholesky | solution.py:36
  314.8 0.2 constant_dynamic-update-slice_fusion.3
  315.0 0.3 convolution_subtract_fusion.3
  315.3 11.7 %cholesky.147 = f32[128,128]{1,0:T(8,128)S(1)} custom-call(f32[128,128]{1,0:T(8,128)S(1)} %convolution_subtract_fusion.3), custom_call_target="Cholesky" | custom-call | tf_op jit(solution)/shard_map/jit(cholesky)/cholesky | solution.py:36
  327.0 0.7 compare_reduce_fusion.2
  329.0 0.1 triangular_solve.75
  329.1 4.2 while.4
  329.3 0.6 fusion.55
  329.9 1.4 bitcast_dynamic-update-slice_fusion.4
  331.3 0.6 fusion.55
  331.9 1.4 bitcast_dynamic-update-slice_fusion.4
  333.3 19.7 %custom-call.14 = f32[2,128,128]{1,2,0:T(8,128)S(1)} custom-call(f32[2,128,128]{2,1,0:T(8,128)S(1)} %get-tuple-element.18), custom_call_target="InvertDiagBlocksLowerTriangular" | custom-call | tf_op jit(solution)/shard_map/jit(_solve_triangular)/triangular_solve | solution.py:37
  353.0 3.7 fusion.3
  356.7 3.6 convolution_subtract_fusion.1
  360.3 1.9 fusion.17
  362.2 14.2 %fusion = f32[3200,256]{1,0:T(8,128)} fusion(bf16[3200,4096]{1,0:T(8,128)(2,1)} %multiply_convert_fusion, bf16[128,4096]{1,0:T(8,128)(2,1)S(1)} %fusion.17, f32[128,4096]{1,0:T(8,128)S(1)} %fusion.3), kind=kOutput, calls=%fused_computation.9 | convolution fusion | flops 6715080704 | bytes 32636928 | tf_op jit(solution)/shard_map/dot_general | solution.py:19
  376.4 0.0 all-gather.5.cloned.1.call-start
  376.5 45.1 %reduce-scatter.5.cloned.1.call-done = f32[800,256]{1,0:T(8,128)} async-done(((f32[3200,256]{1,0:T(8,128)}), f32[800,256]{1,0:T(8,128)}) %reduce-scatter.5.cloned.1.call-update) | async-done | bytes 819216 | tf_op jit(solution)/shard_map/reduce_scatter | solution.py:18
  421.6 2.1 multiply_convert_fusion.1
  423.7 0.0 all-reduce.10.cloned.1.call-start
  423.7 31.5 %all-gather.5.cloned.1.call-done = bf16[3200,256]{1,0:T(8,128)(2,1)} async-done(((bf16[800,256]{1,0:T(8,128)(2,1)}), bf16[3200,256]{1,0:T(8,128)(2,1)}) %all-gather.5.cloned.1.call-update) | async-done | bytes 1638416 | tf_op jit(solution)/shard_map/all_gather | solution.py:28
  455.3 14.4 %fusion.32 = f32[4096,256]{1,0:T(8,128)} fusion(bf16[3200,4096]{1,0:T(8,128)(2,1)} %multiply_convert_fusion, bf16[3200,256]{1,0:T(8,128)(2,1)} %all-gather.5.cloned.1.call-done), kind=kOutput, calls=%fused_computation.68 | convolution fusion | flops 6710886400 | bytes 32047104 | tf_op jit(solution)/shard_map/dot_general | solution.py:29
  469.7 0.2 all-reduce.12.cloned.1.call-start
  469.9 96.4 %all-reduce.10.cloned.1.call-done = f32[4096,256]{1,0:T(8,128)} async-done(((f32[4096,256]{1,0:T(8,128)}), f32[4096,256]{1,0:T(8,128)}) %all-reduce.10.cloned.1.call-update) | async-done | bytes 4194320 | tf_op jit(solution)/shard_map/psum | solution.py:32
  566.3 10.9 %fusion.33 = f32[256,256]{0,1:T(8,128)} fusion(f32[4096,256]{1,0:T(8,128)} %all-reduce.10.cloned.1.call-done), kind=kOutput, calls=%fused_computation.69 | convolution fusion | flops 3221225472 | bytes 4456448 | tf_op jit(solution)/shard_map/dot_general | solution.py:34
  577.3 43.2 %all-reduce.12.cloned.1.call-done = f32[256,256]{0,1:T(8,128)} async-done(((f32[256,256]{0,1:T(8,128)}), f32[256,256]{0,1:T(8,128)}) %all-reduce.12.cloned.1.call-update) | async-done | bytes 262160 | tf_op jit(solution)/shard_map/psum | solution.py:33
  620.5 1.1 copy.10
  621.6 1.0 fusion.8
  622.6 11.7 %cholesky.164 = f32[128,128]{1,0:T(8,128)S(1)} custom-call(f32[128,128]{1,0:T(8,128)S(1)} %cholesky.197), custom_call_target="Cholesky" | custom-call | tf_op jit(solution)/shard_map/jit(cholesky)/cholesky | solution.py:36
  634.4 10.0 %custom-call.15 = f32[1,128,128]{1,2,0:T(8,128)S(1)} custom-call(f32[1,128,128]{2,1,0:T(8,128)S(1)} %get-tuple-element.47), custom_call_target="InvertDiagBlocksLowerTriangular" | custom-call | tf_op jit(solution)/shard_map/jit(cholesky)/cholesky | solution.py:36
  644.4 0.2 constant_dynamic-update-slice_fusion.1
  644.6 0.3 convolution_subtract_fusion.2
  644.9 11.7 %cholesky.181 = f32[128,128]{1,0:T(8,128)S(1)} custom-call(f32[128,128]{1,0:T(8,128)S(1)} %convolution_subtract_fusion.2), custom_call_target="Cholesky" | custom-call | tf_op jit(solution)/shard_map/jit(cholesky)/cholesky | solution.py:36
  656.6 0.6 compare_reduce_fusion
  657.2 0.6 compare_reduce_fusion.1
  659.2 0.7 fusion.11
  659.9 3.9 while.5
  660.0 0.6 fusion.56
  660.5 1.4 bitcast_dynamic-update-slice_fusion.5
  661.9 0.6 fusion.56
  662.5 1.4 bitcast_dynamic-update-slice_fusion.5
  663.9 19.7 %custom-call.16 = f32[2,128,128]{1,2,0:T(8,128)S(1)} custom-call(f32[2,128,128]{2,1,0:T(8,128)S(1)} %get-tuple-element.19), custom_call_target="InvertDiagBlocksLowerTriangular" | custom-call | tf_op jit(solution)/shard_map/jit(_solve_triangular)/triangular_solve | solution.py:37
  683.6 3.7 fusion.1
  687.3 3.4 convolution_subtract_fusion
  690.7 2.0 fusion.13
  692.7 2.4 maximum_bitcast_fusion
  695.1 5.6 copy.11
  (33 shorter events, 0.5 us)
Async XLA Ops:
  7.2 1.1 copy-start
  7.2 84.8 %reduce-scatter.3.cloned.1.call-start = ((), (), s32[]{:S(2)}) async-start(), calls=%async_computation.2 | async-start | bytes 4096000 | tf_op jit(solution)/shard_map/reduce_scatter | solution.py:18
  44.1 81.7 %all-gather.3.cloned.1.call-start = ((), (), s32[]{:S(2)}) async-start(), calls=%async_computation.3 | async-start | bytes 2048000 | tf_op jit(solution)/shard_map/all_gather | solution.py:28
  94.1 142.8 %all-reduce.6.cloned.1.call-start = ((), (), s32[]{:S(2)}) async-start(), calls=%async_computation.4 | async-start | bytes 8388608 | tf_op jit(solution)/shard_map/psum | solution.py:32
  140.3 150.8 %all-reduce.8.cloned.1.call-start = ((), (), s32[]{:S(2)}) async-start(), calls=%async_computation.5 | async-start | bytes 524288 | tf_op jit(solution)/shard_map/psum | solution.py:33
  247.9 173.7 %reduce-scatter.5.cloned.1.call-start = ((), (), s32[]{:S(2)}) async-start(), calls=%async_computation.6 | async-start | bytes 4096000 | tf_op jit(solution)/shard_map/reduce_scatter | solution.py:18
  353.0 3.7 copy-start.2
  376.4 78.8 %all-gather.5.cloned.1.call-start = ((), (), s32[]{:S(2)}) async-start(), calls=%async_computation.7 | async-start | bytes 2048000 | tf_op jit(solution)/shard_map/all_gather | solution.py:28
  423.7 142.6 %all-reduce.10.cloned.1.call-start = ((), (), s32[]{:S(2)}) async-start(), calls=%async_computation.8 | async-start | bytes 8388608 | tf_op jit(solution)/shard_map/psum | solution.py:32
  469.7 150.8 %all-reduce.12.cloned.1.call-start = ((), (), s32[]{:S(2)}) async-start(), calls=%async_computation.9 | async-start | bytes 524288 | tf_op jit(solution)/shard_map/psum | solution.py:33
  683.6 3.7 copy-start.3
  692.7 8.0 %copy-start.1 = (bf16[64,4096]{1,0:T(8,128)(2,1)S(1)}, bf16[64,4096]{1,0:T(8,128)(2,1)}, u32[]{:S(2)}) copy-start(bf16[64,4096]{1,0:T(8,128)(2,1)} %param.10) | copy-start | bytes 1572868
Sparse Core Ops, SparseCore 0:
  44.3 47.7 reduce-scatter.2
  94.4 31.3 all-gather.2
  140.4 96.4 all-reduce.5
  248.0 43.0 all-reduce.7
  376.6 44.9 reduce-scatter.4
  423.9 31.3 all-gather.4
  469.8 96.4 all-reduce.9
  577.4 43.0 all-reduce.11
where the time goes:
time: 716 us; the launch traced here: 708 us
  waiting for transfers between devices  434 us (61%)
  matrix products  120 us (17%)
  other arithmetic  117 us (16%)
  local copies, waits for them, and re-layouts  17.5 us (2%)
  between operations  17.3 us (2%)
    psum x2, waiting for transfers between devices, per_device(): image_sum = lax.psum(partial_sum, 'img')  193 us
    reduce_scatter x2, waiting for transfers between devices, per_device(): lax.psum_scatter(jnp.dot(filtered, probe_half, preferred_element_type=jnp...  92.2 us
    psum x2, waiting for transfers between devices, per_device(): lax.psum(jnp.dot(image_sum.T, image_sum, precision=lax.Precision.HIGHEST)...  86.3 us
    another operation x13, other arithmetic, per_device(): factor = jnp.linalg.cholesky(gram_matrix)  68.7 us
    all_gather x2, waiting for transfers between devices, per_device(): scaled = lax.all_gather(scaled_share, 'pix', axis=0, tiled=True)  63.2 us
    another operation x5, other arithmetic, per_device(): jax.scipy.linalg.solve_triangular(factor, image_sum.T, lower=True)  40.1 us
    dot_general x2, matrix products, per_device(): lax.dot_general(filtered, scaled, (((0,), (0,)), ((), ())), preferred_ele...  28.8 us
    dot_general x2, matrix products, per_device(): jnp.dot(filtered, probe_half, preferred_element_type=jnp.float32)  28.6 us
  transfers between devices with their start and end apart: 8, of which 8 were waited for; matrix products, arithmetic and copies ran while one was open for 0% of the time, Pallas kernels for 0%

commit v1 on v0

--- a/solution.py
+++ b/solution.py
@@ -29,7 +29,11 @@
         partial_sum = lax.dot_general(
             filtered, scaled, (((0,), (0,)), ((), ())), preferred_element_type=jnp.float32
         )
-        image_sum = lax.psum(partial_sum, "img")
+        image_sum = partial_sum
+        for hop in (1, 2, 4):
+            image_sum = image_sum + lax.ppermute(
+                image_sum, "img", [(dev, dev ^ hop) for dev in range(8)]
+            )
         gram_matrix = lax.psum(
             jnp.dot(image_sum.T, image_sum, precision=lax.Precision.HIGHEST), "pix"
         )

time: 716 us -> 1090 us (1.52)
  waiting for transfers between devices: 434 us -> 787 us
  other arithmetic: 117 us -> 134 us
    ppermute x0 -> x6, waiting for transfers between devices: none -> 557 us  [per_device(): lax.ppermute(image_sum, 'img', [(dev, dev ^ hop) for dev in range(8)])]
    psum x2 -> x0, waiting for transfers between devices: 193 us -> none  [per_device(): image_sum = lax.psum(partial_sum, 'img')]
    psum x2, waiting for transfers between devices: 86.3 us -> 74 us  [per_device(): lax.psum(jnp.dot(image_sum.T, image_sum, precision=lax.Precision.HIGHEST)...]
    transpose x0 -> x2, other arithmetic: none -> 12 us  [per_device(): gram_matrix = lax.psum(jnp.dot(image_sum.T, image_sum, precision=lax.Prec...]
  transfers between devices with their start and end apart: 8 -> 12, of which waited for: 8 -> 12; matrix products, arithmetic and copies ran while one was open for 0% -> 1% of each run, Pallas kernels for 0% -> 0%
where the time goes in v1:
time: 1090 us; the launch traced here: 1080 us
  waiting for transfers between devices  787 us (72%)
  other arithmetic  134 us (12%)
  matrix products  118 us (11%)
  local copies, waits for them, and re-layouts  19.4 us (2%)
  between operations  17.1 us (2%)
    ppermute x6, waiting for transfers between devices, per_device(): lax.ppermute(image_sum, 'img', [(dev, dev ^ hop) for dev in range(8)])  557 us
    reduce_scatter x2, waiting for transfers between devices, per_device(): lax.psum_scatter(jnp.dot(filtered, probe_half, preferred_element_type=jnp...  92.2 us
    psum x2, waiting for transfers between devices, per_device(): lax.psum(jnp.dot(image_sum.T, image_sum, precision=lax.Precision.HIGHEST)...  74 us
    another operation x13, other arithmetic, per_device(): factor = jnp.linalg.cholesky(gram_matrix)  69 us
    all_gather x2, waiting for transfers between devices, per_device(): scaled = lax.all_gather(scaled_share, 'pix', axis=0, tiled=True)  63.2 us
    another operation x5, other arithmetic, per_device(): jax.scipy.linalg.solve_triangular(factor, image_sum.T, lower=True)  40.3 us
    dot_general x2, matrix products, per_device(): jnp.dot(filtered, probe_half, preferred_element_type=jnp.float32)  28.4 us
    dot_general x2, matrix products, per_device(): lax.dot_general(filtered, scaled, (((0,), (0,)), ((), ())), preferred_ele...  27.5 us
  transfers between devices with their start and end apart: 12, of which 12 were waited for; matrix products, arithmetic and copies ran while one was open for 1% of the time, Pallas kernels for 0%

profile of v1, /device:TPU:0, one launch (start us, length us, event | category | flops | bytes accessed | tf_op | source)
XLA Modules:
  0.0 1084.0 jit_solution(1685576016877776053)
XLA Ops:
  7.2 1.0 copy-done
  8.2 21.5 %multiply_convert_fusion = bf16[3200,4096]{1,0:T(8,128)(2,1)} fusion(bf16[3200,4096]{1,0:T(8,128)(2,1)} %param.8, bf16[64,4096]{1,0:T(8,128)(2,1)S(1)} %copy-done, s32[3200]{0:T(1024)} %param.9), kind=kOutput, calls=%fused_computation.4 | convolution fusion | flops 1717248000 | bytes 52965888 | tf_op jit(solution)/shard_map/dot_general | solution.py:11
  29.7 14.4 %fusion.7 = f32[3200,256]{1,0:T(8,128)} fusion(bf16[3200,4096]{1,0:T(8,128)(2,1)} %multiply_convert_fusion, f32[4096,256]{1,0:T(8,128)} %param.12), kind=kOutput, calls=%fused_computation.16 | convolution fusion | flops 6711934976 | bytes 33685504 | tf_op jit(solution)/shard_map/dot_general | solution.py:19
  44.2 0.8 dynamic_slice.4
  45.0 47.0 %reduce-scatter.3.cloned.1.call-done = f32[800,256]{1,0:T(8,128)} async-done(((f32[3200,256]{1,0:T(8,128)}), f32[800,256]{1,0:T(8,128)}) %reduce-scatter.3.cloned.1.call-update) | async-done | bytes 819216 | tf_op jit(solution)/shard_map/reduce_scatter | solution.py:18
  92.0 2.1 multiply_convert_fusion.2
  94.2 31.7 %all-gather.3.cloned.1.call-done = bf16[3200,256]{1,0:T(8,128)(2,1)} async-done(((bf16[800,256]{1,0:T(8,128)(2,1)}), bf16[3200,256]{1,0:T(8,128)(2,1)}) %all-gather.3.cloned.1.call-update) | async-done | bytes 1638416 | tf_op jit(solution)/shard_map/all_gather | solution.py:28
  125.9 13.7 %fusion.36 = f32[4096,256]{1,0:T(8,128)S(1)} fusion(bf16[3200,4096]{1,0:T(8,128)(2,1)} %multiply_convert_fusion, bf16[3200,256]{1,0:T(8,128)(2,1)} %all-gather.3.cloned.1.call-done), kind=kOutput, calls=%fused_computation.74 | convolution fusion | flops 6710886400 | bytes 32047104 | tf_op jit(solution)/shard_map/dot_general | solution.py:29
  139.7 7.1 collective-permute-done
  147.3 1.6 collective-permute-start.1
  148.9 91.1 %collective-permute-done.1 = f32[4096,256]{1,0:T(8,128)S(1)} collective-permute-done((f32[4096,256]{1,0:T(8,128)S(1)}, f32[4096,256]{1,0:T(8,128)S(1)}, u32[]{:S(2)}, u32[]{:S(2)}) %collective-permute-start.1) | collective-permute-done | bytes 4194336 | tf_op jit(solution)/shard_map/ppermute | solution.py:34
  240.0 2.6 add.50
  242.6 2.4 collective-permute-start.2
  245.0 180.4 %collective-permute-done.2 = f32[4096,256]{1,0:T(8,128)} collective-permute-done((f32[4096,256]{1,0:T(8,128)}, f32[4096,256]{1,0:T(8,128)}, u32[]{:S(2)}, u32[]{:S(2)}) %collective-permute-start.2) | collective-permute-done | bytes 4194336 | tf_op jit(solution)/shard_map/ppermute | solution.py:34
  425.4 13.5 %fusion.11 = f32[256,256]{0,1:T(8,128)} fusion(f32[4096,256]{1,0:T(8,128)} %add.50, f32[4096,256]{1,0:T(8,128)} %collective-permute-done.2), kind=kOutput, calls=%fused_computation.22 | convolution fusion | flops 3222274048 | bytes 8650752 | tf_op jit(solution)/shard_map/dot_general | solution.py:38
  439.2 6.0 add_bitcast_fusion.1
  445.2 36.9 %all-reduce.4.cloned.1.call-done = f32[256,256]{0,1:T(8,128)} async-done(((f32[256,256]{0,1:T(8,128)}), f32[256,256]{0,1:T(8,128)}) %all-reduce.4.cloned.1.call-update) | async-done | bytes 262160 | tf_op jit(solution)/shard_map/psum | solution.py:37
  482.1 1.1 copy.8
  483.2 1.0 fusion.15
  484.2 11.7 %cholesky.130 = f32[128,128]{1,0:T(8,128)S(1)} custom-call(f32[128,128]{1,0:T(8,128)S(1)} %cholesky.194), custom_call_target="Cholesky" | custom-call | tf_op jit(solution)/shard_map/jit(cholesky)/cholesky | solution.py:40
  496.0 9.8 custom-call.13
  506.3 11.7 %cholesky.147 = f32[128,128]{1,0:T(8,128)S(1)} custom-call(f32[128,128]{1,0:T(8,128)S(1)} %convolution_subtract_fusion.1), custom_call_target="Cholesky" | custom-call | tf_op jit(solution)/shard_map/jit(cholesky)/cholesky | solution.py:40
  518.0 0.6 compare_reduce_fusion.2
  520.0 4.2 while.4
  521.0 1.3 bitcast_dynamic-update-slice_fusion.4
  522.4 0.6 fusion.53
  522.9 1.3 bitcast_dynamic-update-slice_fusion.4
  524.3 19.7 %custom-call.14 = f32[2,128,128]{1,2,0:T(8,128)S(1)} custom-call(f32[2,128,128]{2,1,0:T(8,128)S(1)} %get-tuple-element.18), custom_call_target="InvertDiagBlocksLowerTriangular" | custom-call | tf_op jit(solution)/shard_map/jit(_solve_triangular)/triangular_solve | solution.py:41
  543.9 3.7 fusion.5
  547.6 3.5 fusion.22
  551.2 2.0 fusion.4
  553.2 14.0 %fusion = f32[3200,256]{1,0:T(8,128)} fusion(bf16[3200,4096]{1,0:T(8,128)(2,1)} %multiply_convert_fusion, bf16[128,4096]{1,0:T(8,128)(2,1)S(1)} %fusion.4, f32[128,4096]{1,0:T(8,128)S(1)} %fusion.5), kind=kOutput, calls=%fused_computation.7 | convolution fusion | flops 6715080704 | bytes 32636928 | tf_op jit(solution)/shard_map/dot_general | solution.py:19
  567.2 45.1 %reduce-scatter.5.cloned.1.call-done = f32[800,256]{1,0:T(8,128)} async-done(((f32[3200,256]{1,0:T(8,128)}), f32[800,256]{1,0:T(8,128)}) %reduce-scatter.5.cloned.1.call-update) | async-done | bytes 819216 | tf_op jit(solution)/shard_map/reduce_scatter | solution.py:18
  612.3 2.1 multiply_convert_fusion.1
  614.5 31.5 %all-gather.5.cloned.1.call-done = bf16[3200,256]{1,0:T(8,128)(2,1)} async-done(((bf16[800,256]{1,0:T(8,128)(2,1)}), bf16[3200,256]{1,0:T(8,128)(2,1)}) %all-gather.5.cloned.1.call-update) | async-done | bytes 1638416 | tf_op jit(solution)/shard_map/all_gather | solution.py:28
  646.0 13.7 %fusion.37 = f32[4096,256]{1,0:T(8,128)S(1)} fusion(bf16[3200,4096]{1,0:T(8,128)(2,1)} %multiply_convert_fusion, bf16[3200,256]{1,0:T(8,128)(2,1)} %all-gather.5.cloned.1.call-done), kind=kOutput, calls=%fused_computation.75 | convolution fusion | flops 6710886400 | bytes 32047104 | tf_op jit(solution)/shard_map/dot_general | solution.py:29
  659.8 7.1 collective-permute-done.3
  667.5 1.6 collective-permute-start.4
  669.1 91.1 %collective-permute-done.4 = f32[4096,256]{1,0:T(8,128)S(1)} collective-permute-done((f32[4096,256]{1,0:T(8,128)S(1)}, f32[4096,256]{1,0:T(8,128)S(1)}, u32[]{:S(2)}, u32[]{:S(2)}) %collective-permute-start.4) | collective-permute-done | bytes 4194336 | tf_op jit(solution)/shard_map/ppermute | solution.py:34
  760.8 2.5 collective-permute-start.5
  763.2 180.1 %collective-permute-done.5 = f32[4096,256]{1,0:T(8,128)S(1)} collective-permute-done((f32[4096,256]{1,0:T(8,128)S(1)}, f32[4096,256]{1,0:T(8,128)S(1)}, u32[]{:S(2)}, u32[]{:S(2)}) %collective-permute-start.5) | collective-permute-done | bytes 4194336 | tf_op jit(solution)/shard_map/ppermute | solution.py:34
  943.4 1.9 copy-done.4
  945.3 7.6 fusion.9
  952.9 6.0 add_bitcast_fusion
  959.0 37.1 %all-reduce.6.cloned.1.call-done = f32[256,256]{0,1:T(8,128)} async-done(((f32[256,256]{0,1:T(8,128)}), f32[256,256]{0,1:T(8,128)}) %all-reduce.6.cloned.1.call-update) | async-done | bytes 262160 | tf_op jit(solution)/shard_map/psum | solution.py:37
  996.1 1.1 copy.10
  997.2 1.0 fusion.14
  998.2 12.1 %cholesky.164 = f32[128,128]{1,0:T(8,128)S(1)} custom-call(f32[128,128]{1,0:T(8,128)S(1)} %cholesky.197), custom_call_target="Cholesky" | custom-call | tf_op jit(solution)/shard_map/jit(cholesky)/cholesky | solution.py:40
  1010.3 9.8 custom-call.15
  1020.6 11.7 %cholesky.181 = f32[128,128]{1,0:T(8,128)S(1)} custom-call(f32[128,128]{1,0:T(8,128)S(1)} %convolution_subtract_fusion), custom_call_target="Cholesky" | custom-call | tf_op jit(solution)/shard_map/jit(cholesky)/cholesky | solution.py:40
  1032.4 0.7 compare_reduce_fusion
  1033.1 0.6 compare_reduce_fusion.1
  1035.1 0.7 fusion.17
  1035.8 4.1 while.5
  1035.8 0.7 fusion.54
  1036.5 1.3 bitcast_dynamic-update-slice_fusion.5
  1037.9 0.7 fusion.54
  1038.5 1.3 bitcast_dynamic-update-slice_fusion.5
  1039.9 19.8 %custom-call.16 = f32[2,128,128]{1,2,0:T(8,128)S(1)} custom-call(f32[2,128,128]{2,1,0:T(8,128)S(1)} %get-tuple-element.19), custom_call_target="InvertDiagBlocksLowerTriangular" | custom-call | tf_op jit(solution)/shard_map/jit(_solve_triangular)/triangular_solve | solution.py:41
  1059.8 3.7 fusion.2
  1063.5 3.4 fusion.18
  1066.9 2.0 fusion.1
  1068.9 2.4 maximum_bitcast_fusion
  1071.4 5.6 copy.11
  (49 shorter events, 4.2 us)
Async XLA Ops:
  7.2 1.1 copy-start
  7.2 84.8 %reduce-scatter.3.cloned.1.call-start = ((), (), s32[]{:S(2)}) async-start(), calls=%async_computation.2 | async-start | bytes 4096000 | tf_op jit(solution)/shard_map/reduce_scatter | solution.py:18
  44.1 81.7 %all-gather.3.cloned.1.call-start = ((), (), s32[]{:S(2)}) async-start(), calls=%async_computation.3 | async-start | bytes 2048000 | tf_op jit(solution)/shard_map/all_gather | solution.py:28
  94.1 388.0 %all-reduce.4.cloned.1.call-start = ((), (), s32[]{:S(2)}) async-start(), calls=%async_computation.4 | async-start | bytes 524288 | tf_op jit(solution)/shard_map/psum | solution.py:37
  139.6 7.2 collective-permute-start
  147.3 92.7 %collective-permute-start.1 = (f32[4096,256]{1,0:T(8,128)S(1)}, f32[4096,256]{1,0:T(8,128)S(1)}, u32[]{:S(2)}, u32[]{:S(2)}) collective-permute-start(f32[4096,256]{1,0:T(8,128)S(1)} %add.49), channel_id=1, source_target_pairs={{0,8},{4,12},{8,0},{12,4},{16,24},{20,28},{24,16},{28,20},{1,9},{5... | collective-permute-start | bytes 12582920 | tf_op jit(solution)/shard_map/ppermute | solution.py:34
  242.6 182.9 %collective-permute-start.2 = (f32[4096,256]{1,0:T(8,128)}, f32[4096,256]{1,0:T(8,128)}, u32[]{:S(2)}, u32[]{:S(2)}) collective-permute-start(f32[4096,256]{1,0:T(8,128)} %add.50), channel_id=1, source_target_pairs={{0,16},{4,20},{8,24},{12,28},{16,0},{20,4},{24,8},{28,12},{1,17},{... | collective-permute-start | bytes 12582920 | tf_op jit(solution)/shard_map/ppermute | solution.py:34
  438.9 173.4 %reduce-scatter.5.cloned.1.call-start = ((), (), s32[]{:S(2)}) async-start(), calls=%async_computation.5 | async-start | bytes 4096000 | tf_op jit(solution)/shard_map/reduce_scatter | solution.py:18
  543.9 7.2 copy-start.5
  567.2 78.8 %all-gather.5.cloned.1.call-start = ((), (), s32[]{:S(2)}) async-start(), calls=%async_computation.6 | async-start | bytes 2048000 | tf_op jit(solution)/shard_map/all_gather | solution.py:28
  614.4 381.7 %all-reduce.6.cloned.1.call-start = ((), (), s32[]{:S(2)}) async-start(), calls=%async_computation.7 | async-start | bytes 524288 | tf_op jit(solution)/shard_map/psum | solution.py:37
  659.8 7.2 collective-permute-start.3
  667.5 92.7 %collective-permute-start.4 = (f32[4096,256]{1,0:T(8,128)S(1)}, f32[4096,256]{1,0:T(8,128)S(1)}, u32[]{:S(2)}, u32[]{:S(2)}) collective-permute-start(f32[4096,256]{1,0:T(8,128)S(1)} %add.52), channel_id=1, source_target_pairs={{0,8},{4,12},{8,0},{12,4},{16,24},{20,28},{24,16},{28,20},{1,9},{5... | collective-permute-start | bytes 12582920 | tf_op jit(solution)/shard_map/ppermute | solution.py:34
  760.8 182.6 %copy-start.2 = (f32[4096,256]{1,0:T(8,128)}, f32[4096,256]{1,0:T(8,128)S(1)}, u32[]{:S(2)}) copy-start(f32[4096,256]{1,0:T(8,128)S(1)} %add.53) | copy-start | bytes 12582916
  760.8 182.6 %collective-permute-start.5 = (f32[4096,256]{1,0:T(8,128)S(1)}, f32[4096,256]{1,0:T(8,128)S(1)}, u32[]{:S(2)}, u32[]{:S(2)}) collective-permute-start(f32[4096,256]{1,0:T(8,128)S(1)} %add.53), channel_id=1, source_target_pairs={{0,16},{4,20},{8,24},{12,28},{16,0},{20,4},{24,8},{28,12},{1,17},{... | collective-permute-start | bytes 12582920 | tf_op jit(solution)/shard_map/ppermute | solution.py:34
  943.4 1.9 copy-start.4
  1059.8 7.1 copy-start.3
  1068.9 8.0 copy-start.1
Sparse Core Ops, SparseCore 0:
  44.3 47.7 reduce-scatter.2
  94.4 31.3 all-gather.2
  439.1 43.0 all-reduce.3
  567.3 44.9 reduce-scatter.4
  614.6 31.3 all-gather.4
  953.1 42.9 all-reduce.5
